TPU v7x, 256 devices: a whole 4x4x8 slice. The times are simulated.
256 devices in a mesh: dom: 64 (over x, z, y_hi), head: 4 (over y_lo, core).
Axes of the slice: x: 4, y: 4 (y_hi: 2, y_lo: 2; y = y_hi * 2 + y_lo), z: 8, core: 2. Of those that a mesh axis runs over, the one named last changes fastest.
Arguments:
- vertex_embeddings: bfloat16 [32768, 512], P(('dom', 'head')), may hold values from -6 to 6
- adjacent_group_bank_ids: int32 [64, 4, 12], P('dom', 'head'), may hold values from -1 to 15, as said below
- coupling_strength_panels: bfloat16 [16, 128, 128], replicated, may hold values from -0.3125 to 0.3125
- asking_projector: bfloat16 [512, 512], replicated, may hold values from -0.25 to 0.25
- lookup_projector: bfloat16 [512, 512], replicated, may hold values from -0.25 to 0.25
- content_projector: bfloat16 [512, 512], replicated, may hold values from -0.25 to 0.25
- final_projector: bfloat16 [512, 512], replicated, may hold values from -0.25 to 0.25
- passing_inner_coefficients: bfloat16 [512, 1024], replicated, may hold values from -0.25 to 0.25
- passing_outer_coefficients: bfloat16 [1024, 512], replicated, may hold values from -0.1875 to 0.1875
- softness_per_subspace: float32 [8], replicated, may hold values from 0.5 to 2
- mixing_layer_gain: float32 [512], replicated, may hold values from 0.5 to 1.5
Outputs:
- result: bfloat16 [32768, 512], P(('dom', 'head'))
Inputs may be any that keep to these rules, and one draw needn't show every extreme that they name: `adjacent_group_bank_ids`: -1 marks a block without edges. The entry of a block for itself is never -1, nor is at least one entry for each neighbouring partition.
All inputs are finite; a program needn't handle non-finite values.
Results may differ from a plain program's by a relative error of at most 0.0054.
Values may be sent and summed in bfloat16 or wider, within the bound.
A program may use at most 64 MiB of HBM per device.

v0:
```python
import math
import jax
import jax.numpy as jnp
from jax import lax
from jax.sharding import PartitionSpec as P

NUM_SUBSPACES = 8
SUBSPACE_WIDTH = 64
norm_eps = 1e-06


def extended(shard, sides, width):
    for axis, dim in sides:
        devices, length = (lax.axis_size(axis), shard.shape[dim])
        up = [(i, (i + 1) % devices) for i in range(devices - 1)]
        down = [(j, i) for i, j in up]
        last = lax.slice_in_dim(shard, length - width, length, axis=dim)
        first = lax.slice_in_dim(shard, 0, width, axis=dim)
        before = lax.ppermute(last, axis, up)
        after = lax.ppermute(first, axis, down)
        shard = jnp.concatenate([before, shard, after], axis=dim)
    return shard


def head_norm(projected, scales):
    rows = projected.shape[0]
    grouped = projected.reshape(rows, -1, SUBSPACE_WIDTH)
    mean_square = jnp.mean(grouped * grouped, axis=-1, keepdims=True)
    scaled = grouped * lax.rsqrt(mean_square + norm_eps)
    if scales is not None:
        scaled = scaled * scales[None, :, None]
    return scaled.reshape(rows, -1).astype(jnp.bfloat16)


def shards(
    vertex_embeddings,
    adjacent_group_bank_ids,
    coupling_strength_panels,
    asking_projector,
    lookup_projector,
    content_projector,
    final_projector,
    passing_inner_coefficients,
    passing_outer_coefficients,
    softness_per_subspace,
    mixing_layer_gain,
):
    block_len = vertex_embeddings.shape[0]
    group_size = lax.axis_size("head")
    heads_here = NUM_SUBSPACES // group_size
    head_cols = heads_here * SUBSPACE_WIDTH
    slot_ids = adjacent_group_bank_ids.reshape(-1)
    halo_rows = extended(vertex_embeddings, (("dom", 0),), block_len)
    nearby = lax.all_gather(halo_rows, "head", axis=0, tiled=True)
    slot_order = slot_ids.reshape(3, group_size).T.reshape(-1)
    asking_vector_multiplier = softness_per_subspace / math.sqrt(SUBSPACE_WIDTH)
    queries = head_norm(
        jnp.dot(vertex_embeddings, asking_projector, preferred_element_type=jnp.float32),
        asking_vector_multiplier,
    )
    keys_all = head_norm(
        jnp.dot(vertex_embeddings, lookup_projector, preferred_element_type=jnp.float32), None
    )
    values_all = jnp.dot(
        vertex_embeddings, content_projector, preferred_element_type=jnp.float32
    ).astype(jnp.bfloat16)
    queries, keys_all, values_all = (
        lax.all_to_all(queries, "head", split_axis=1, concat_axis=0, tiled=True),
        lax.all_to_all(keys_all, "head", split_axis=1, concat_axis=0, tiled=True),
        lax.all_to_all(values_all, "head", split_axis=1, concat_axis=0, tiled=True),
    )
    selected = jnp.take(coupling_strength_panels, jnp.maximum(slot_order, 0), axis=0)
    selected = jnp.where((slot_order >= 0)[:, None, None], selected, jnp.zeros_like(selected))
    wide_tiles = jnp.transpose(selected, (1, 0, 2)).reshape(block_len, -1)
    aggregate = jnp.dot(wide_tiles, nearby, preferred_element_type=jnp.float32).astype(jnp.bfloat16)
    hidden = jax.nn.gelu(
        jnp.dot(aggregate, passing_inner_coefficients, preferred_element_type=jnp.float32)
    ).astype(jnp.bfloat16)
    local_term = jnp.dot(hidden, passing_outer_coefficients, preferred_element_type=jnp.float32)
    query_rows = queries.shape[0]
    start_totals = (
        jnp.zeros((query_rows, head_cols), jnp.float32),
        jnp.zeros((query_rows, heads_here), jnp.float32),
    )
    keys_in = lax.all_gather(keys_all, "dom", axis=0, tiled=True)
    values_in = lax.all_gather(values_all, "dom", axis=0, tiled=True)
    key_count = keys_in.shape[0]
    block_step = key_count
    while block_step > 2048 and block_step % 2 == 0:
        block_step = block_step // 2

    def accumulate(turn_index, totals):
        numerator, denominator = totals
        key_block = lax.dynamic_slice_in_dim(keys_in, turn_index * block_step, block_step, 0)
        value_block = lax.dynamic_slice_in_dim(values_in, turn_index * block_step, block_step, 0)
        new_numer = []
        new_denom = []
        for head_id in range(heads_here):
            cols = slice(head_id * SUBSPACE_WIDTH, (head_id + 1) * SUBSPACE_WIDTH)
            scores = jnp.einsum(
                "qd,kd->qk",
                queries[:, cols],
                key_block[:, cols],
                preferred_element_type=jnp.float32,
            )
            weights = jnp.exp(scores).astype(jnp.bfloat16)
            new_denom.append(jnp.sum(weights, axis=1, dtype=jnp.float32))
            new_numer.append(
                jnp.dot(weights, value_block[:, cols], preferred_element_type=jnp.float32)
            )
        return (
            numerator + jnp.concatenate(new_numer, axis=1),
            denominator + jnp.stack(new_denom, axis=1),
        )

    numerator, denominator = lax.fori_loop(0, key_count // block_step, accumulate, start_totals)
    merged = (
        (numerator.reshape(query_rows, heads_here, SUBSPACE_WIDTH) / denominator[:, :, None])
        .reshape(query_rows, head_cols)
        .astype(jnp.bfloat16)
    )
    node_heads = lax.all_to_all(merged, "head", split_axis=0, concat_axis=1, tiled=True)
    attended = jnp.dot(node_heads, final_projector, preferred_element_type=jnp.float32)
    normed = (
        attended
        * lax.rsqrt(jnp.mean(attended * attended, axis=-1, keepdims=True) + norm_eps)
        * mixing_layer_gain
    )
    return (vertex_embeddings.astype(jnp.float32) + local_term + normed).astype(jnp.bfloat16)


def solution(mesh):
    in_specs = (
        P(("dom", "head"), None),
        P("dom", "head", None),
        P(),
        P(),
        P(),
        P(),
        P(),
        P(),
        P(),
        P(),
        P(),
    )
    out_specs = P(("dom", "head"), None)
    return jax.shard_map(shards, mesh=mesh, in_specs=in_specs, out_specs=out_specs, check_vma=False)
```

profile of v0, /device:TPU:1, one launch (start us, length us, event | category | flops | bytes accessed | tf_op | source)
XLA Modules:
  0.0 446.1 jit_solution(16894264735324568818)
XLA Ops:
  8.4 9.9 %all_to_all.76 = bf16[128,4,128]{2,0,1:T(8,128)(2,1)} all-to-all(bf16[128,4,128]{2,0,1:T(8,128)(2,1)S(1)} %copy_bitcast_fusion.2), channel_id=1, replica_groups=mesh['dom'=64,'head'=4] {'head'}, dimensions={1} | all-to-all | bytes 262144 | tf_op jit(solution)/shard_map/all_to_all | solution.py:69
  19.8 7.7 %all_to_all.77 = bf16[128,4,128]{2,0,1:T(8,128)(2,1)} all-to-all(bf16[128,4,128]{2,0,1:T(8,128)(2,1)S(1)} %bitcast.74), channel_id=1, replica_groups=mesh['dom'=64,'head'=4] {'head'}, dimensions={1} | all-to-all | bytes 262144 | tf_op jit(solution)/shard_map/all_to_all | solution.py:70
  27.5 3.1 collective-permute-start
  33.3 4.6 %all-to-all-start.1 = ((bf16[128,4,128]{2,0,1:T(8,128)(2,1)}), bf16[128,4,128]{2,0,1:T(8,128)(2,1)S(1)}, u32[]{:S(2)}, u32[]{:S(2)}) async-start(bf16[128,4,128]{2,0,1:T(8,128)(2,1)} %copy_bitcast_fusion.1), calls=%async_computation.1 | async-start | bytes 262144 | tf_op jit(solution)/shard_map/all_to_all | solution.py:68
  42.0 122.8 %all-gather.6.cloned.1.call-done = bf16[32768,128]{1,0:T(8,128)(2,1)} async-done(((bf16[512,128]{1,0:T(8,128)(2,1)}), bf16[32768,128]{1,0:T(8,128)(2,1)}) %all-gather.6.cloned.1.call-update) | async-done | bytes 8388624 | tf_op jit(solution)/shard_map/all_gather | solution.py:85
  164.7 147.5 %all-gather.8.cloned.1.call-done = bf16[32768,128]{1,0:T(8,128)(2,1)} async-done(((bf16[512,128]{1,0:T(8,128)(2,1)}), bf16[32768,128]{1,0:T(8,128)(2,1)}) %all-gather.8.cloned.1.call-update) | async-done | bytes 8388624 | tf_op jit(solution)/shard_map/all_gather | solution.py:86
  312.2 114.2 %while.16 = (s32[]{:T(128)}, f32[512,128]{0,1:T(8,128)S(1)}, f32[512,2]{0,1:T(2,128)S(1)}, bf16[32768,128]{1,0:T(8,128)(2,1)}, bf16[512,128]{1,0:T(8,128)(2,1)S(...) while((s32[]{:T(128)}, f32[512,128]{0,1:T(8,128)S(1)}, ...), condition=%wide.region_5.6_spmd.clone, body=%wide.region_2.5_spmd.clone.sunk | while | flops 543361024 | bytes 11813066 | solution.py:116
  312.2 1.9 convert_reduce_fusion.4
  314.1 1.7 fusion.54
  315.9 1.8 convert_reduce_fusion.5
  317.6 1.6 fusion.55
  319.3 1.9 convert_reduce_fusion.4
  321.3 1.7 fusion.54
  323.0 1.8 convert_reduce_fusion.5
  324.8 1.6 fusion.55
  326.5 1.9 convert_reduce_fusion.4
  328.4 1.7 fusion.54
  330.2 1.8 convert_reduce_fusion.5
  333.7 1.9 convert_reduce_fusion.4
  335.6 1.7 fusion.54
  337.3 1.8 convert_reduce_fusion.5
  339.1 1.6 fusion.55
  340.8 1.9 convert_reduce_fusion.4
  342.7 1.7 fusion.54
  344.5 1.8 convert_reduce_fusion.5
  346.2 1.6 fusion.55
  347.9 1.9 convert_reduce_fusion.4
  349.9 1.7 fusion.54
  351.6 1.8 convert_reduce_fusion.5
  353.4 1.6 fusion.55
  355.1 1.9 convert_reduce_fusion.4
  357.0 1.7 fusion.54
  358.7 1.8 convert_reduce_fusion.5
  360.5 1.6 fusion.55
  362.2 1.9 convert_reduce_fusion.4
  364.1 1.7 fusion.54
  365.9 1.8 convert_reduce_fusion.5
  369.3 1.9 convert_reduce_fusion.4
  371.3 1.7 fusion.54
  373.0 1.8 convert_reduce_fusion.5
  376.5 1.9 convert_reduce_fusion.4
  378.4 1.7 fusion.54
  380.1 1.8 convert_reduce_fusion.5
  383.6 1.9 convert_reduce_fusion.4
  385.5 1.7 fusion.54
  387.2 1.8 convert_reduce_fusion.5
  390.7 1.9 convert_reduce_fusion.4
  392.7 1.7 fusion.54
  394.4 1.8 convert_reduce_fusion.5
  397.9 1.9 convert_reduce_fusion.4
  399.8 1.7 fusion.54
  401.5 1.8 convert_reduce_fusion.5
  405.0 1.9 convert_reduce_fusion.4
  406.9 1.7 fusion.54
  408.6 1.8 convert_reduce_fusion.5
  412.1 1.9 convert_reduce_fusion.4
  414.1 1.7 fusion.54
  415.8 1.8 convert_reduce_fusion.5
  419.3 1.9 convert_reduce_fusion.4
  421.2 1.7 fusion.54
  422.9 1.8 convert_reduce_fusion.5
  427.2 6.4 %all-to-all-start.3 = ((bf16[4,128,128]{2,1,0:T(8,128)(2,1)}), bf16[4,128,128]{2,1,0:T(8,128)(2,1)S(1)}, u32[]{:S(2)}, u32[]{:S(2)}) async-start(bf16[4,128,128]{2,1,0:T(8,128)(2,1)} %bitcast.16), calls=%async_computation.3 | async-start | bytes 262144 | tf_op jit(solution)/shard_map/all_to_all | solution.py:122
  433.6 2.8 fusion.21
  437.7 1.9 fusion.11
  (114 shorter events, 29.2 us)
Async XLA Ops:
  6.5 427.0 %copy-start = (bf16[512,1024]{1,0:T(8,128)(2,1)S(1)}, bf16[512,1024]{1,0:T(8,128)(2,1)}, u32[]{:S(2)}) copy-start(bf16[512,1024]{1,0:T(8,128)(2,1)} %param.20) | copy-start | bytes 3145732
  6.5 20.9 %copy-start.1 = (bf16[128,512]{1,0:T(8,128)(2,1)S(1)}, bf16[128,512]{1,0:T(8,128)(2,1)}, u32[]{:S(2)}) copy-start(bf16[128,512]{1,0:T(8,128)(2,1)} %param.13) | copy-start | bytes 393220
  6.5 25.4 %copy-start.3 = (bf16[512,512]{1,0:T(8,128)(2,1)S(1)}, bf16[512,512]{1,0:T(8,128)(2,1)}, u32[]{:S(2)}) copy-start(bf16[512,512]{1,0:T(8,128)(2,1)} %param.16) | copy-start | bytes 1572868
  6.5 25.9 %copy-start.7 = (f32[8]{0:T(128)S(1)}, f32[8]{0:T(128)}, u32[]{:S(2)}) copy-start(f32[8]{0:T(128)} %param.22) | copy-start | bytes 100
  6.5 158.2 %all-gather.6.cloned.1.call-start = ((), (), s32[]{:S(2)}) async-start(), calls=%async_computation.5 | async-start | bytes 8519680 | tf_op jit(solution)/shard_map/all_gather | solution.py:85
  8.0 29.9 %copy-start.8 = (s32[1,1,12]{2,1,0:T(1,128)S(1)}, s32[1,1,12]{2,1,0:T(1,128)}, u32[]{:S(2)}) copy-start(s32[1,1,12]{2,1,0:T(1,128)} %param.14) | copy-start | bytes 148
  8.1 30.8 %copy-start.5 = (bf16[16,128,128]{2,1,0:T(8,128)(2,1)S(1)}, bf16[16,128,128]{2,1,0:T(8,128)(2,1)}, u32[]{:S(2)}) copy-start(bf16[16,128,128]{2,1,0:T(8,128)(2,1)} %param.15) | copy-start | bytes 1572868
  18.3 293.9 %all-gather.8.cloned.1.call-start = ((), (), s32[]{:S(2)}) async-start(), calls=%async_computation.6 | async-start | bytes 8519680 | tf_op jit(solution)/shard_map/all_gather | solution.py:86
  27.5 12.4 %collective-permute-start = (bf16[128,512]{1,0:T(8,128)(2,1)S(1)}, bf16[128,512]{1,0:T(8,128)(2,1)S(1)}, u32[]{:S(2)}, u32[]{:S(2)}) collective-permute-start(bf16[128,512]{1,0:T(8,128)(2,1)S(1)} %copy-done.1), channel_id=1, source_target_pairs={{0,4},{4,8},{8,12},{12,16},{16,20},{20,24},{24,28},{28,32},{32,36}... | collective-permute-start | bytes 393224 | tf_op jit(solution)/shard_map/ppermute | solution.py:19
  30.6 9.3 %collective-permute-start.1 = (bf16[128,512]{1,0:T(8,128)(2,1)S(1)}, bf16[128,512]{1,0:T(8,128)(2,1)S(1)}, u32[]{:S(2)}, u32[]{:S(2)}) collective-permute-start(bf16[128,512]{1,0:T(8,128)(2,1)S(1)} %copy-done.1), channel_id=1, source_target_pairs={{4,0},{8,4},{12,8},{16,12},{20,16},{24,20},{28,24},{32,28},{36,32}... | collective-permute-start | bytes 393224 | tf_op jit(solution)/shard_map/ppermute | solution.py:20
  33.3 8.6 %all-to-all-start.1 = ((bf16[128,4,128]{2,0,1:T(8,128)(2,1)}), bf16[128,4,128]{2,0,1:T(8,128)(2,1)S(1)}, u32[]{:S(2)}, u32[]{:S(2)}) async-start(bf16[128,4,128]{2,0,1:T(8,128)(2,1)} %copy_bitcast_fusion.1), calls=%async_computation.1 | async-start | bytes 262144 | tf_op jit(solution)/shard_map/all_to_all | solution.py:68
  38.0 395.6 %all-gather.4.cloned.1.call-start = ((), (), s32[]{:S(2)}) async-start(), calls=%async_computation.4 | async-start | bytes 1966080 | tf_op jit(solution)/shard_map/all_gather | solution.py:54
  426.4 10.9 %copy-start.4 = (bf16[512,512]{1,0:T(8,128)(2,1)S(1)}, bf16[512,512]{1,0:T(8,128)(2,1)}, u32[]{:S(2)}) copy-start(bf16[512,512]{1,0:T(8,128)(2,1)} %param.19) | copy-start | bytes 1572868
  426.4 11.3 %copy-start.2 = (bf16[1024,512]{1,0:T(8,128)(2,1)S(1)}, bf16[1024,512]{1,0:T(8,128)(2,1)}, u32[]{:S(2)}) copy-start(bf16[1024,512]{1,0:T(8,128)(2,1)} %param.21) | copy-start | bytes 3145732
  426.4 11.3 %copy-start.6 = (f32[512]{0:T(512)S(1)}, f32[512]{0:T(512)}, u32[]{:S(2)}) copy-start(f32[512]{0:T(512)} %param.23) | copy-start | bytes 6148
  427.2 10.0 %all-to-all-start.3 = ((bf16[4,128,128]{2,1,0:T(8,128)(2,1)}), bf16[4,128,128]{2,1,0:T(8,128)(2,1)S(1)}, u32[]{:S(2)}, u32[]{:S(2)}) async-start(bf16[4,128,128]{2,1,0:T(8,128)(2,1)} %bitcast.16), calls=%async_computation.3 | async-start | bytes 262144 | tf_op jit(solution)/shard_map/all_to_all | solution.py:122
Sparse Core Ops, SparseCore 0:
  18.5 146.2 all-gather.5
  168.3 143.8 all-gather.7
  314.0 26.9 all-gather.3
where the time goes:
time: 450 us; the launch traced here: 446 us
  waiting for transfers between devices  272 us (60%)
  matrix products  120 us (27%)
  blocking collectives  17.5 us (4%)
  starting transfers between devices  15.4 us (3%)
  between operations  13.4 us (3%)
    all_gather x1, waiting for transfers between devices, shards(): values_in = lax.all_gather(values_all, 'dom', axis=0, tiled=True)  147 us
    all_gather x1, waiting for transfers between devices, shards(): keys_in = lax.all_gather(keys_all, 'dom', axis=0, tiled=True)  123 us
    dot_general x32, matrix products, accumulate(): jnp.einsum('qd,kd->qk', queries[:, cols], key_block[:, cols], preferred_e...  59.1 us
    dot_general x32, matrix products, accumulate(): jnp.dot(weights, value_block[:, cols], preferred_element_type=jnp.float32)  52.5 us
    all_to_all x1, blocking collectives, shards(): lax.all_to_all(keys_all, 'head', split_axis=1, concat_axis=0, tiled=True)  9.87 us
  transfers between devices with their start and end apart: 7, of which 4 were waited for; matrix products, arithmetic and copies ran while one was open for 27% of the time, Pallas kernels for 0%

commit v1 on v0

--- a/solution.py
+++ b/solution.py
@@ -83,7 +83,8 @@
         jnp.zeros((query_rows, heads_here), jnp.float32),
     )
     keys_in = lax.all_gather(keys_all, "dom", axis=0, tiled=True)
-    values_in = lax.all_gather(values_all, "dom", axis=0, tiled=True)
+    sent = jnp.stack([values_all] * lax.axis_size("dom"))
+    values_in = jnp.concatenate(lax.all_to_all(sent, "dom", 0, 0), axis=0)
     key_count = keys_in.shape[0]
     block_step = key_count
     while block_step > 2048 and block_step % 2 == 0:

time: 450 us -> 412 us (0.916)
  waiting for transfers between devices: 272 us -> 221 us
  starting transfers between devices: 15.4 us -> 38 us
  blocking collectives: 17.5 us -> 0 us
  local copies, waits for them, and re-layouts: 3.34 us -> 9.24 us
    all_gather x1 -> x0, waiting for transfers between devices: 147 us -> none  [shards(): values_in = lax.all_gather(values_all, 'dom', axis=0, tiled=True)]
    all_gather x1, waiting for transfers between devices: 123 us -> 195 us  [shards(): keys_in = lax.all_gather(keys_all, 'dom', axis=0, tiled=True)]
    all_to_all x0 -> x3, starting transfers between devices: none -> 21.6 us  [the longest x1 12.9 us: shards(): values_in = jnp.concatenate(lax.all_to_all(sent, 'dom', 0, 0), axis=0)]
    all_to_all x2 -> x0, blocking collectives: 17.5 us -> none  [the longest x1 9.87 us: shards(): lax.all_to_all(keys_all, 'head', split_axis=1, concat_axis=0, tiled=True)]
    ppermute x1, waiting for transfers between devices: 0.01 us -> 11.8 us  [extended(): before = lax.ppermute(last, axis, up)]
    ppermute x1, waiting for transfers between devices: 0.01 us -> 5.55 us  [extended(): after = lax.ppermute(first, axis, down)]
    all_to_all x0 -> x3, waiting for transfers between devices: none -> 5.55 us  [the longest x1 2.88 us: shards(): lax.all_to_all(values_all, 'head', split_axis=1, concat_axis=0, tiled=True)]
    another operation x0 -> x1, local copies, waits for them, and re-layouts: none -> 5.24 us  [shards(): sent = jnp.stack([values_all] * lax.axis_size('dom'))]
  transfers between devices with their start and end apart: 7 -> 9, of which waited for: 4 -> 7; matrix products, arithmetic and copies ran while one was open for 27% -> 31% of each run, Pallas kernels for 0% -> 0%
where the time goes in v1:
time: 412 us; the launch traced here: 407 us
  waiting for transfers between devices  221 us (54%)
  matrix products  120 us (29%)
  starting transfers between devices  38 us (9%)
  between operations  13.7 us (3%)
  local copies, waits for them, and re-layouts  9.24 us (2%)
  other arithmetic  4.78 us (1%)
    all_gather x1, waiting for transfers between devices, shards(): keys_in = lax.all_gather(keys_all, 'dom', axis=0, tiled=True)  195 us
    dot_general x32, matrix products, accumulate(): jnp.einsum('qd,kd->qk', queries[:, cols], key_block[:, cols], preferred_e...  59 us
    dot_general x32, matrix products, accumulate(): jnp.dot(weights, value_block[:, cols], preferred_element_type=jnp.float32)  52.6 us
    all_to_all x1, starting transfers between devices, shards(): values_in = jnp.concatenate(lax.all_to_all(sent, 'dom', 0, 0), axis=0)  12.9 us
    ppermute x1, waiting for transfers between devices, extended(): before = lax.ppermute(last, axis, up)  11.8 us
  transfers between devices with their start and end apart: 9, of which 7 were waited for; matrix products, arithmetic and copies ran while one was open for 31% of the time, Pallas kernels for 0%

profile of v1, /device:TPU:1, one launch (start us, length us, event | category | flops | bytes accessed | tf_op | source)
XLA Modules:
  0.0 407.0 jit_solution(6640386290506742570)
XLA Ops:
  9.8 6.5 %all-to-all-start.1 = ((bf16[128,4,128]{2,0,1:T(8,128)(2,1)}), bf16[128,4,128]{2,0,1:T(8,128)(2,1)S(1)}, u32[]{:S(2)}, u32[]{:S(2)}) async-start(bf16[128,4,128]{2,0,1:T(8,128)(2,1)} %copy_bitcast_fusion.1), calls=%async_computation.1 | async-start | bytes 262144 | tf_op jit(solution)/shard_map/all_to_all | solution.py:68
  20.0 4.3 %all-to-all-start = ((bf16[128,4,128]{2,0,1:T(8,128)(2,1)}), bf16[128,4,128]{2,0,1:T(8,128)(2,1)S(1)}, u32[]{:S(2)}, u32[]{:S(2)}) async-start(bf16[128,4,128]{2,0,1:T(8,128)(2,1)} %copy_bitcast_fusion.2), calls=%async_computation | async-start | bytes 262144 | tf_op jit(solution)/shard_map/all_to_all | solution.py:69
  25.2 2.7 all-to-all-done
  27.9 4.3 %all-to-all-start.2 = ((bf16[128,4,128]{2,0,1:T(8,128)(2,1)}), bf16[128,4,128]{2,0,1:T(8,128)(2,1)S(1)}, u32[]{:S(2)}, u32[]{:S(2)}) async-start(bf16[128,4,128]{2,0,1:T(8,128)(2,1)} %bitcast.60), calls=%async_computation.2 | async-start | bytes 262144 | tf_op jit(solution)/shard_map/all_to_all | solution.py:70
  33.0 2.9 all-to-all-done.2
  35.8 5.2 %stack.23 = bf16[64,512,128]{2,1,0:T(8,128)(2,1)} broadcast(bf16[512,128]{1,0:T(8,128)(2,1)S(1)} %bitcast.71), dimensions={1,2} | broadcast | bytes 8519680 | tf_op jit(solution)/shard_map/stack | solution.py:86
  41.1 12.9 %all-to-all-start.3 = ((bf16[64,512,128]{2,1,0:T(8,128)(2,1)}), bf16[64,512,128]{2,1,0:T(8,128)(2,1)}, u32[]{:S(2)}, u32[]{:S(2)}) async-start(bf16[64,512,128]{2,1,0:T(8,128)(2,1)} %stack.23), calls=%async_computation.3 | async-start | bytes 16777216 | tf_op jit(solution)/shard_map/all_to_all | solution.py:87
  54.1 4.4 %collective-permute-start = (bf16[128,512]{1,0:T(8,128)(2,1)S(1)}, bf16[128,512]{1,0:T(8,128)(2,1)S(1)}, u32[]{:S(2)}, u32[]{:S(2)}) collective-permute-start(bf16[128,512]{1,0:T(8,128)(2,1)S(1)} %copy-done.1), channel_id=1, source_target_pairs={{0,4},{4,8},{8,12},{12,16},{16,20},{20,24},{24,28},{28,32},{32,36}... | collective-permute-start | bytes 393224 | tf_op jit(solution)/shard_map/ppermute | solution.py:19
  61.7 11.8 %collective-permute-done = bf16[128,512]{1,0:T(8,128)(2,1)S(1)} collective-permute-done((bf16[128,512]{1,0:T(8,128)(2,1)S(1)}, bf16[128,512]{1,0:T(8,128)(2,1)S(1)}, u32[]{:S(2)}, u32[]{:S(2)}) %collective-permute-start) | collective-permute-done | bytes 131104 | tf_op jit(solution)/shard_map/ppermute | solution.py:19
  73.5 5.6 %collective-permute-done.1 = bf16[128,512]{1,0:T(8,128)(2,1)S(1)} collective-permute-done((bf16[128,512]{1,0:T(8,128)(2,1)S(1)}, bf16[128,512]{1,0:T(8,128)(2,1)S(1)}, u32[]{:S(2)}, u32[]{:S(2)}) %collective-permute-start.1) | collective-permute-done | bytes 131104 | tf_op jit(solution)/shard_map/ppermute | solution.py:20
  79.8 195.2 %all-gather.5.cloned.1.call-done = bf16[32768,128]{1,0:T(8,128)(2,1)} async-done(((bf16[512,128]{1,0:T(8,128)(2,1)}), bf16[32768,128]{1,0:T(8,128)(2,1)}) %all-gather.5.cloned.1.call-update) | async-done | bytes 8388624 | tf_op jit(solution)/shard_map/all_gather | solution.py:85
  275.0 114.0 %while.16 = (s32[]{:T(128)}, f32[512,128]{0,1:T(8,128)S(1)}, f32[512,2]{0,1:T(2,128)S(1)}, bf16[32768,128]{1,0:T(8,128)(2,1)}, bf16[512,128]{1,0:T(8,128)(2,1)S(...) while((s32[]{:T(128)}, f32[512,128]{0,1:T(8,128)S(1)}, ...), condition=%wide.region_5.6_spmd.clone, body=%wide.region_2.5_spmd.clone.sunk | while | flops 543361024 | bytes 11813066 | solution.py:117
  275.0 1.9 convert_reduce_fusion.4
  276.9 1.7 fusion.54
  278.6 1.8 convert_reduce_fusion.5
  282.1 1.9 convert_reduce_fusion.4
  284.0 1.7 fusion.54
  285.7 1.8 convert_reduce_fusion.5
  287.5 1.6 fusion.55
  289.2 1.9 convert_reduce_fusion.4
  291.2 1.7 fusion.54
  292.9 1.8 convert_reduce_fusion.5
  296.4 1.9 convert_reduce_fusion.4
  298.3 1.7 fusion.54
  300.1 1.8 convert_reduce_fusion.5
  303.5 1.9 convert_reduce_fusion.4
  305.5 1.7 fusion.54
  307.2 1.8 convert_reduce_fusion.5
  310.7 1.9 convert_reduce_fusion.4
  312.6 1.7 fusion.54
  314.3 1.8 convert_reduce_fusion.5
  317.8 1.9 convert_reduce_fusion.4
  319.7 1.7 fusion.54
  321.4 1.8 convert_reduce_fusion.5
  324.9 1.9 convert_reduce_fusion.4
  326.8 1.7 fusion.54
  328.6 1.8 convert_reduce_fusion.5
  332.0 1.9 convert_reduce_fusion.4
  334.0 1.7 fusion.54
  335.7 1.8 convert_reduce_fusion.5
  339.2 1.9 convert_reduce_fusion.4
  341.1 1.7 fusion.54
  342.8 1.8 convert_reduce_fusion.5
  346.3 1.9 convert_reduce_fusion.4
  348.2 1.7 fusion.54
  349.9 1.8 convert_reduce_fusion.5
  353.4 1.9 convert_reduce_fusion.4
  355.3 1.7 fusion.54
  357.1 1.8 convert_reduce_fusion.5
  360.5 1.9 convert_reduce_fusion.4
  362.4 1.7 fusion.54
  364.2 1.8 convert_reduce_fusion.5
  367.7 1.9 convert_reduce_fusion.4
  369.6 1.7 fusion.54
  371.3 1.8 convert_reduce_fusion.5
  374.8 1.9 convert_reduce_fusion.4
  376.7 1.7 fusion.54
  378.4 1.8 convert_reduce_fusion.5
  381.9 1.9 convert_reduce_fusion.4
  383.8 1.7 fusion.54
  385.6 1.8 convert_reduce_fusion.5
  389.8 4.2 %all-to-all-start.4 = ((bf16[4,128,128]{2,1,0:T(8,128)(2,1)}), bf16[4,128,128]{2,1,0:T(8,128)(2,1)S(1)}, u32[]{:S(2)}, u32[]{:S(2)}) async-start(bf16[4,128,128]{2,1,0:T(8,128)(2,1)} %bitcast.17), calls=%async_computation.4 | async-start | bytes 262144 | tf_op jit(solution)/shard_map/all_to_all | solution.py:123
  394.1 2.8 fusion.21
  398.2 1.9 fusion.11
  (116 shorter events, 39.7 us)
Async XLA Ops:
  6.5 387.5 %copy-start = (bf16[512,1024]{1,0:T(8,128)(2,1)S(1)}, bf16[512,1024]{1,0:T(8,128)(2,1)}, u32[]{:S(2)}) copy-start(bf16[512,1024]{1,0:T(8,128)(2,1)} %param.20) | copy-start | bytes 3145732
  6.5 17.8 %copy-start.1 = (bf16[128,512]{1,0:T(8,128)(2,1)S(1)}, bf16[128,512]{1,0:T(8,128)(2,1)}, u32[]{:S(2)}) copy-start(bf16[128,512]{1,0:T(8,128)(2,1)} %param.13) | copy-start | bytes 393220
  6.5 17.8 %copy-start.3 = (bf16[512,512]{1,0:T(8,128)(2,1)S(1)}, bf16[512,512]{1,0:T(8,128)(2,1)}, u32[]{:S(2)}) copy-start(bf16[512,512]{1,0:T(8,128)(2,1)} %param.18) | copy-start | bytes 1572868
  9.8 10.1 %all-to-all-start.1 = ((bf16[128,4,128]{2,0,1:T(8,128)(2,1)}), bf16[128,4,128]{2,0,1:T(8,128)(2,1)S(1)}, u32[]{:S(2)}, u32[]{:S(2)}) async-start(bf16[128,4,128]{2,0,1:T(8,128)(2,1)} %copy_bitcast_fusion.1), calls=%async_computation.1 | async-start | bytes 262144 | tf_op jit(solution)/shard_map/all_to_all | solution.py:68
  20.0 7.9 %all-to-all-start = ((bf16[128,4,128]{2,0,1:T(8,128)(2,1)}), bf16[128,4,128]{2,0,1:T(8,128)(2,1)S(1)}, u32[]{:S(2)}, u32[]{:S(2)}) async-start(bf16[128,4,128]{2,0,1:T(8,128)(2,1)} %copy_bitcast_fusion.2), calls=%async_computation | async-start | bytes 262144 | tf_op jit(solution)/shard_map/all_to_all | solution.py:69
  27.9 4.3 %copy-start.5 = (bf16[128,4,128]{2,0,1:T(8,128)(2,1)}, bf16[128,4,128]{2,0,1:T(8,128)(2,1)S(1)}, u32[]{:S(2)}) copy-start(bf16[128,4,128]{2,0,1:T(8,128)(2,1)S(1)} %all-to-all-done) | copy-start | bytes 393220
  27.9 7.9 %all-to-all-start.2 = ((bf16[128,4,128]{2,0,1:T(8,128)(2,1)}), bf16[128,4,128]{2,0,1:T(8,128)(2,1)S(1)}, u32[]{:S(2)}, u32[]{:S(2)}) async-start(bf16[128,4,128]{2,0,1:T(8,128)(2,1)} %bitcast.60), calls=%async_computation.2 | async-start | bytes 262144 | tf_op jit(solution)/shard_map/all_to_all | solution.py:70
  32.2 242.7 %all-gather.5.cloned.1.call-start = ((), (), s32[]{:S(2)}) async-start(), calls=%async_computation.6 | async-start | bytes 8519680 | tf_op jit(solution)/shard_map/all_gather | solution.py:85
  41.1 18.7 %copy-start.8 = (s32[1,1,12]{2,1,0:T(1,128)S(1)}, s32[1,1,12]{2,1,0:T(1,128)}, u32[]{:S(2)}) copy-start(s32[1,1,12]{2,1,0:T(1,128)} %param.14) | copy-start | bytes 148
  41.1 19.6 %copy-start.6 = (bf16[16,128,128]{2,1,0:T(8,128)(2,1)S(1)}, bf16[16,128,128]{2,1,0:T(8,128)(2,1)}, u32[]{:S(2)}) copy-start(bf16[16,128,128]{2,1,0:T(8,128)(2,1)} %param.15) | copy-start | bytes 1572868
  41.1 233.9 %all-to-all-start.3 = ((bf16[64,512,128]{2,1,0:T(8,128)(2,1)}), bf16[64,512,128]{2,1,0:T(8,128)(2,1)}, u32[]{:S(2)}, u32[]{:S(2)}) async-start(bf16[64,512,128]{2,1,0:T(8,128)(2,1)} %stack.23), calls=%async_computation.3 | async-start | bytes 16777216 | tf_op jit(solution)/shard_map/all_to_all | solution.py:87
  54.0 340.0 %all-gather.3.cloned.1.call-start = ((), (), s32[]{:S(2)}) async-start(), calls=%async_computation.5 | async-start | bytes 1966080 | tf_op jit(solution)/shard_map/all_gather | solution.py:54
  54.1 19.4 %collective-permute-start = (bf16[128,512]{1,0:T(8,128)(2,1)S(1)}, bf16[128,512]{1,0:T(8,128)(2,1)S(1)}, u32[]{:S(2)}, u32[]{:S(2)}) collective-permute-start(bf16[128,512]{1,0:T(8,128)(2,1)S(1)} %copy-done.1), channel_id=1, source_target_pairs={{0,4},{4,8},{8,12},{12,16},{16,20},{20,24},{24,28},{28,32},{32,36}... | collective-permute-start | bytes 393224 | tf_op jit(solution)/shard_map/ppermute | solution.py:19
  58.4 20.6 %collective-permute-start.1 = (bf16[128,512]{1,0:T(8,128)(2,1)S(1)}, bf16[128,512]{1,0:T(8,128)(2,1)S(1)}, u32[]{:S(2)}, u32[]{:S(2)}) collective-permute-start(bf16[128,512]{1,0:T(8,128)(2,1)S(1)} %copy-done.1), channel_id=1, source_target_pairs={{4,0},{8,4},{12,8},{16,12},{20,16},{24,20},{28,24},{32,28},{36,32}... | collective-permute-start | bytes 393224 | tf_op jit(solution)/shard_map/ppermute | solution.py:20
  389.0 8.8 %copy-start.4 = (bf16[512,512]{1,0:T(8,128)(2,1)S(1)}, bf16[512,512]{1,0:T(8,128)(2,1)}, u32[]{:S(2)}) copy-start(bf16[512,512]{1,0:T(8,128)(2,1)} %param.19) | copy-start | bytes 1572868
  389.0 9.1 %copy-start.2 = (bf16[1024,512]{1,0:T(8,128)(2,1)S(1)}, bf16[1024,512]{1,0:T(8,128)(2,1)}, u32[]{:S(2)}) copy-start(bf16[1024,512]{1,0:T(8,128)(2,1)} %param.21) | copy-start | bytes 3145732
  389.0 9.1 %copy-start.7 = (f32[512]{0:T(512)S(1)}, f32[512]{0:T(512)}, u32[]{:S(2)}) copy-start(f32[512]{0:T(512)} %param.23) | copy-start | bytes 6148
  389.8 7.8 %all-to-all-start.4 = ((bf16[4,128,128]{2,1,0:T(8,128)(2,1)}), bf16[4,128,128]{2,1,0:T(8,128)(2,1)S(1)}, u32[]{:S(2)}, u32[]{:S(2)}) async-start(bf16[4,128,128]{2,1,0:T(8,128)(2,1)} %bitcast.17), calls=%async_computation.4 | async-start | bytes 262144 | tf_op jit(solution)/shard_map/all_to_all | solution.py:123
Sparse Core Ops, SparseCore 0:
  36.7 238.2 all-gather.4
  276.8 28.0 all-gather.2
